TPU v7x, 256 devices: a whole 4x4x8 slice. The times are simulated.
256 devices in a mesh: ctx: 32 (over z_hi, x, y), fsdp: 8 (over z_lo, core).
Axes of the slice: x: 4, y: 4, z: 8 (z_hi: 2, z_lo: 4; z = z_hi * 4 + z_lo), core: 2. Of those that a mesh axis runs over, the one named last changes fastest.
Arguments:
- out_grad: bfloat16 [4096, 32768], P('fsdp', 'ctx'), may hold values from -6 to 6
- gate_values: bfloat16 [4096, 32768], P('fsdp', 'ctx'), may hold values from -6 to 6
- kv_product: bfloat16 [4096, 32768], P('fsdp', 'ctx'), may hold values from -6 to 6
- w_out: bfloat16 [4096, 4096], P('ctx', 'fsdp'), may hold values from -0.09375 to 0.09375
- filters: bfloat16 [8, 32, 16, 128], P('fsdp', 'ctx'), may hold values from -0.5 to 0.5
Outputs:
- gate_grad: float32 [4096, 32768], P('fsdp', 'ctx')
- kv_grad: bfloat16 [4096, 32768], P('fsdp', 'ctx')
- filter_grad: float32 [8, 32, 16, 128], P('fsdp', 'ctx')
- w_grad: float32 [4096, 4096], P('ctx', 'fsdp')
All inputs are finite; a program needn't handle non-finite values.
Results may differ from a plain program's by a relative error of at most 0.0049.
Values may be sent and summed in bfloat16 or wider, within the bound.
A program may use at most 128 MiB of HBM per device.

v0:
```python
import math
import jax
import jax.numpy as jnp
from jax import lax
from jax.sharding import PartitionSpec as P


def toeplitz_pair(filters):
    channels, tap_count = filters.shape
    zero_pad = jnp.zeros_like(filters)

    def make_band(vector):
        tiled = jnp.tile(vector, (1, tap_count + 1))
        window_cut = tiled[:, tap_count : tap_count + tap_count * (2 * tap_count - 1)]
        return window_cut.reshape(channels, tap_count, 2 * tap_count - 1)[:, :, :tap_count]

    near_band = make_band(jnp.concatenate([zero_pad, filters], axis=1))
    far_band = make_band(jnp.concatenate([filters, zero_pad], axis=1))
    return (near_band, far_band)


def mixer_piece(filters, signal, signal_prior, cotangent, cotangent_after):
    channels, seq_len = signal.shape
    tap_count = filters.shape[1]
    blocks_count = seq_len // tap_count
    near_band, far_band = toeplitz_pair(filters)
    current = signal.reshape(channels, blocks_count, tap_count)
    previous = jnp.concatenate([signal_prior[:, None, :], current[:, :-1]], axis=1)
    grad_current = cotangent.reshape(channels, blocks_count, tap_count)
    grad_later = jnp.concatenate([grad_current[:, 1:], cotangent_after[:, None, :]], axis=1)
    wide = jnp.float32
    mixed = jnp.einsum("cbs,csr->cbr", current, near_band, preferred_element_type=wide)
    mixed = mixed + jnp.einsum("cbs,csr->cbr", previous, far_band, preferred_element_type=wide)
    signal_grad = jnp.einsum("cbr,csr->cbs", grad_current, near_band, preferred_element_type=wide)
    signal_grad = signal_grad + jnp.einsum(
        "cbr,csr->cbs", grad_later, far_band, preferred_element_type=wide
    )
    near_weight = jnp.einsum("cbs,cbr->csr", current, grad_current, preferred_element_type=wide)
    far_weight = jnp.einsum("cbs,cbr->csr", previous, grad_current, preferred_element_type=wide)
    band_pair, pullback = jax.vjp(toeplitz_pair, filters.astype(jnp.float32))
    filter_part = pullback((near_weight, far_weight))[0]
    return (mixed.reshape(channels, seq_len), signal_grad.reshape(channels, seq_len), filter_part)


def on_device(out_grad, gate_values, kv_product, w_out, filters):
    ctx_count = lax.axis_size("ctx")
    chan_count = filters.shape[2]
    tap_count = filters.shape[3]
    norm_scale = 1.0 / math.sqrt(ctx_count * out_grad.shape[1])
    grad_full = lax.all_gather(out_grad, "fsdp", axis=0, tiled=True)
    grad_part = grad_full
    mix_grad = lax.dot_general(
        lax.all_gather(w_out, "ctx", axis=0, tiled=True),
        grad_part,
        (((0,), (0,)), ((), ())),
        preferred_element_type=jnp.float32,
    )
    conv_grad = (mix_grad * gate_values.astype(jnp.float32)).astype(jnp.bfloat16)
    signal_chan, grad_chan = (
        lax.all_to_all(kv_product, "ctx", split_axis=0, concat_axis=1, tiled=True),
        lax.all_to_all(conv_grad, "ctx", split_axis=0, concat_axis=1, tiled=True),
    )
    own_filters = filters.reshape(chan_count, tap_count)
    edge_zero = jnp.zeros((chan_count, tap_count), jnp.bfloat16)
    mixed, signal_grad, filter_part = mixer_piece(
        own_filters, signal_chan, edge_zero, grad_chan, edge_zero
    )
    mixed_tok, kv_grad = (
        lax.all_to_all(mixed.astype(jnp.bfloat16), "ctx", split_axis=1, concat_axis=0, tiled=True),
        lax.all_to_all(
            signal_grad.astype(jnp.bfloat16), "ctx", split_axis=1, concat_axis=0, tiled=True
        ),
    )
    filter_grad = (filter_part * norm_scale).reshape(filters.shape)
    mixed_wide = mixed_tok.astype(jnp.float32)
    gate_grad = mix_grad * mixed_wide
    gated_rows = (gate_values.astype(jnp.float32) * mixed_wide).astype(jnp.bfloat16)
    grad_part = grad_full
    w_grad = (
        lax.psum_scatter(
            lax.dot_general(
                grad_part, gated_rows, (((1,), (1,)), ((), ())), preferred_element_type=jnp.float32
            ),
            "ctx",
            scatter_dimension=0,
            tiled=True,
        )
        * norm_scale
    )
    return (gate_grad, kv_grad, filter_grad, w_grad)


def solution(mesh):
    in_specs = (
        P("fsdp", "ctx"),
        P("fsdp", "ctx"),
        P("fsdp", "ctx"),
        P("ctx", "fsdp"),
        P("fsdp", "ctx", None, None),
    )
    out_specs = (P("fsdp", "ctx"), P("fsdp", "ctx"), P("fsdp", "ctx", None, None), P("ctx", "fsdp"))
    return jax.shard_map(
        on_device, mesh=mesh, in_specs=in_specs, out_specs=out_specs, check_vma=False
    )
```

profile of v0, /device:TPU:32, one launch (start us, length us, event | category | flops | bytes accessed | tf_op | source)
XLA Modules:
  0.0 575.9 jit_solution(2997700983290757412)
XLA Ops:
  8.7 13.1 %all-to-all-start = ((bf16[32,16,1024]{2,1,0:T(8,128)(2,1)}), bf16[32,16,1024]{2,1,0:T(8,128)(2,1)S(1)}, u32[]{:S(2)}, u32[]{:S(2)}) async-start(bf16[32,16,1024]{2,1,0:T(8,128)(2,1)} %bitcast.45), calls=%async_computation | async-start | bytes 2097152 | tf_op jit(solution)/shard_map/all_to_all | solution.py:60
  22.2 3.4 reshape.73
  26.9 4.6 reshape.71
  31.5 23.4 %all-to-all-done = bf16[32,16,1024]{2,1,0:T(8,128)(2,1)S(1)} async-done(((bf16[32,16,1024]{2,1,0:T(8,128)(2,1)}), bf16[32,16,1024]{2,1,0:T(8,128)(2,1)S(1)}, u32[]{:S(2)}, u32[]{:S(2)}) %all-to-all-start) | async-done | bytes 1048608 | tf_op jit(solution)/shard_map/all_to_all | solution.py:60
  60.0 1.6 copy.32
  62.9 1.8 copy.33
  64.7 31.7 %all_to_all.58 = bf16[16,32,1024]{2,0,1:T(8,128)(2,1)} all-to-all(bf16[16,32,1024]{2,0,1:T(8,128)(2,1)S(1)} %copy.33), channel_id=1, replica_groups=mesh['ctx'=32,'fsdp'=8] {'ctx'}, dimensions={1} | all-to-all | bytes 2097152 | tf_op jit(solution)/shard_map/all_to_all | solution.py:69
  96.5 51.4 %all-gather.3.cloned.1.call-done = bf16[4096,512]{1,0:T(8,128)(2,1)} async-done(((bf16[128,512]{1,0:T(8,128)(2,1)}), bf16[4096,512]{1,0:T(8,128)(2,1)}) %all-gather.3.cloned.1.call-update) | async-done | bytes 4194320 | tf_op jit(solution)/shard_map/all_gather | solution.py:53
  147.9 86.7 %all-gather.5.cloned.1.call-done = bf16[4096,1024]{1,0:T(8,128)(2,1)} async-done(((bf16[512,1024]{1,0:T(8,128)(2,1)}), bf16[4096,1024]{1,0:T(8,128)(2,1)}) %all-gather.5.cloned.1.call-update) | async-done | bytes 8388624 | tf_op jit(solution)/shard_map/all_gather | solution.py:50
  234.6 11.6 %fusion = (bf16[512,1024]{1,0:T(8,128)(2,1)}, f32[512,1024]{1,0:T(8,128)}, bf16[512,1024]{1,0:T(8,128)(2,1)S(1)}) fusion(bf16[512,1024]{1,0:T(8,128)(2,1)} %param.6, bf16[16,32,1024]{2,0,1:T(8,128)(2,1)} %all_to_all.58, bf16[4096,512]{1,0:T(8,128)(2,1)} %all-gather.3.cloned.1.call-done, bf16[4096,1024]{1,0:T(8,128)(2,1)} %all-gather.5.cloned.1.call-done), kind=kOutput, calls=%fused_computation.3 | convolution fusion | flops 4298637312 | bytes 18874368 | tf_op jit(solution)/shard_map/dot_general | solution.py:52
  246.2 6.9 %convolution_bitcast_fusion = f32[4096,512]{0,1:T(8,128)} fusion(bf16[512,1024]{1,0:T(8,128)(2,1)S(1)} %get-tuple-element.18, bf16[4096,1024]{1,0:T(8,128)(2,1)S(1)} %copy-done.3), kind=kOutput, calls=%fused_computation | convolution fusion | flops 4294967296 | bytes 17825792 | tf_op jit(solution)/shard_map/dot_general | solution.py:81
  253.1 59.1 %all_to_all.59 = bf16[32,16,1024]{2,1,0:T(8,128)(2,1)S(1)} all-to-all(bf16[32,16,1024]{2,1,0:T(8,128)(2,1)} %bitcast.46), channel_id=1, replica_groups=mesh['ctx'=32,'fsdp'=8] {'ctx'}, dimensions={0} | all-to-all | bytes 2097152 | tf_op jit(solution)/shard_map/all_to_all | solution.py:61
  321.4 5.2 all-to-all-start.3
  328.5 2.8 pad.18.clone
  331.3 4.2 reshape.77
  335.4 3.0 pad.19
  338.5 2.9 reshape.78
  341.3 1.8 reduce_sum.19
  343.9 2.6 reshape.75
  346.5 3.1 pad.17
  349.5 1.7 reshape.76
  352.1 3.0 all-to-all-done.3
  355.0 210.2 %reduce-scatter.2.cloned.1.call-done = f32[128,512]{0,1:T(8,128)} async-done(((f32[4096,512]{0,1:T(8,128)}), f32[128,512]{0,1:T(8,128)}) %reduce-scatter.2.cloned.1.call-update) | async-done | bytes 262160 | tf_op jit(solution)/shard_map/reduce_scatter | solution.py:80
  567.1 2.3 copy.50
  (41 shorter events, 23.9 us)
Async XLA Ops:
  7.2 14.6 %copy-start.2 = (bf16[1,1,16,128]{3,2,1,0:T(8,128)(2,1)S(1)}, bf16[1,1,16,128]{3,2,1,0:T(8,128)(2,1)}, u32[]{:S(2)}) copy-start(bf16[1,1,16,128]{3,2,1,0:T(8,128)(2,1)} %param.9) | copy-start | bytes 12292
  7.2 140.7 %all-gather.3.cloned.1.call-start = ((), (), s32[]{:S(2)}) async-start(), calls=%async_computation.5 | async-start | bytes 4325376 | tf_op jit(solution)/shard_map/all_gather | solution.py:53
  7.9 226.7 %all-gather.5.cloned.1.call-start = ((), (), s32[]{:S(2)}) async-start(), calls=%async_computation.6 | async-start | bytes 9437184 | tf_op jit(solution)/shard_map/all_gather | solution.py:50
  8.7 46.3 %all-to-all-start = ((bf16[32,16,1024]{2,1,0:T(8,128)(2,1)}), bf16[32,16,1024]{2,1,0:T(8,128)(2,1)S(1)}, u32[]{:S(2)}, u32[]{:S(2)}) async-start(bf16[32,16,1024]{2,1,0:T(8,128)(2,1)} %bitcast.45), calls=%async_computation | async-start | bytes 2097152 | tf_op jit(solution)/shard_map/all_to_all | solution.py:60
  21.7 543.6 %reduce-scatter.2.cloned.1.call-start = ((), (), s32[]{:S(2)}) async-start(), calls=%async_computation.7 | async-start | bytes 8650752 | tf_op jit(solution)/shard_map/reduce_scatter | solution.py:80
  31.5 27.0 %copy-start = (bf16[16,128,255]{2,1,0:T(8,128)(2,1)}, bf16[16,128,255]{2,1,0:T(8,128)(2,1)S(1)}, u32[]{:S(2)}) copy-start(bf16[16,128,255]{2,1,0:T(8,128)(2,1)S(1)} %reshape.71) | copy-start | bytes 3133444
  234.6 11.6 %copy-start.3 = (bf16[4096,1024]{1,0:T(8,128)(2,1)S(1)}, bf16[4096,1024]{1,0:T(8,128)(2,1)}, u32[]{:S(2)}) copy-start(bf16[4096,1024]{1,0:T(8,128)(2,1)} %all-gather.5.cloned.1.call-done) | copy-start | bytes 25165828
  315.3 1.2 copy-start.1
  321.4 33.6 %all-to-all-start.3 = ((bf16[16,32,1024]{2,0,1:T(8,128)(2,1)}), bf16[16,32,1024]{2,0,1:T(8,128)(2,1)}, u32[]{:S(2)}, u32[]{:S(2)}) async-start(bf16[16,32,1024]{2,0,1:T(8,128)(2,1)} %copy.36), calls=%async_computation.3 | async-start | bytes 2097152 | tf_op jit(solution)/shard_map/all_to_all | solution.py:70
Sparse Core Ops, SparseCore 0:
  11.5 136.3 all-gather.2
  149.7 84.8 all-gather.4
  253.2 312.0 reduce-scatter.1
where the time goes:
time: 577 us; the launch traced here: 576 us
  waiting for transfers between devices  376 us (65%)
  blocking collectives  90.8 us (16%)
  local copies, waits for them, and re-layouts  49.6 us (9%)
  matrix products  23.3 us (4%)
  starting transfers between devices  18.4 us (3%)
  between operations  14 us (2%)
    reduce_scatter x1, waiting for transfers between devices, on_device(): lax.psum_scatter(lax.dot_general(grad_part, gated_rows, (((1,), (1,)), ((...  210 us
    all_gather x1, waiting for transfers between devices, on_device(): grad_full = lax.all_gather(out_grad, 'fsdp', axis=0, tiled=True)  86.7 us
    all_to_all x1, blocking collectives, on_device(): lax.all_to_all(conv_grad, 'ctx', split_axis=0, concat_axis=1, tiled=True)  59.1 us
    all_gather x1, waiting for transfers between devices, on_device(): lax.all_gather(w_out, 'ctx', axis=0, tiled=True)  51.4 us
    all_to_all x1, blocking collectives, on_device(): lax.all_to_all(mixed.astype(jnp.bfloat16), 'ctx', split_axis=1, concat_ax...  31.7 us
    all_to_all x1, waiting for transfers between devices, on_device(): lax.all_to_all(kv_product, 'ctx', split_axis=0, concat_axis=1, tiled=True)  23.4 us
    reshape x4, local copies, waits for them, and re-layouts, make_band(): window_cut.reshape(channels, tap_count, 2 * tap_count - 1)[:, :, :tap_count]  14.7 us
    all_to_all x1, starting transfers between devices, on_device(): lax.all_to_all(kv_product, 'ctx', split_axis=0, concat_axis=1, tiled=True)  13.1 us
  transfers between devices with their start and end apart: 5, of which 5 were waited for; matrix products, arithmetic and copies ran while one was open for 9% of the time, Pallas kernels for 0%

commit v1 on v0

--- a/solution.py
+++ b/solution.py
@@ -66,7 +66,15 @@
         own_filters, signal_chan, edge_zero, grad_chan, edge_zero
     )
     mixed_tok, kv_grad = (
-        lax.all_to_all(mixed.astype(jnp.bfloat16), "ctx", split_axis=1, concat_axis=0, tiled=True),
+        jnp.concatenate(
+            lax.all_to_all(
+                jnp.stack(jnp.split(mixed.astype(jnp.bfloat16), lax.axis_size("ctx"), axis=1)),
+                "ctx",
+                0,
+                0,
+            ),
+            axis=0,
+        ),
         lax.all_to_all(
             signal_grad.astype(jnp.bfloat16), "ctx", split_axis=1, concat_axis=0, tiled=True
         ),

time: 577 us -> 558 us (0.967)
  waiting for transfers between devices: 376 us -> 341 us
  blocking collectives: 90.8 us -> 99 us
    all_gather x1, waiting for transfers between devices: 86.7 us -> 30.9 us  [on_device(): grad_full = lax.all_gather(out_grad, 'fsdp', axis=0, tiled=True)]
    all_gather x1, waiting for transfers between devices: 51.4 us -> 105 us  [on_device(): lax.all_gather(w_out, 'ctx', axis=0, tiled=True)]
    reduce_scatter x1, waiting for transfers between devices: 210 us -> 158 us  [on_device(): lax.psum_scatter(lax.dot_general(grad_part, gated_rows, (((1,), (1,)), ((...]
    all_to_all x1, blocking collectives: 31.7 us -> 44.9 us  [on_device(): lax.all_to_all(jnp.stack(jnp.split(mixed.astype(jnp.bfloat16), lax.axis_s...]
    all_to_all x1, waiting for transfers between devices: 2.97 us -> 15 us  [on_device(): lax.all_to_all(signal_grad.astype(jnp.bfloat16), 'ctx', split_axis=1, con...]
    all_to_all x1, waiting for transfers between devices: 23.4 us -> 31.2 us  [on_device(): lax.all_to_all(kv_product, 'ctx', split_axis=0, concat_axis=1, tiled=True)]
  transfers between devices with their start and end apart: 5 -> 5, of which waited for: 5 -> 5; matrix products, arithmetic and copies ran while one was open for 9% -> 13% of each run, Pallas kernels for 0% -> 0%
where the time goes in v1:
time: 558 us; the launch traced here: 552 us
  waiting for transfers between devices  341 us (61%)
  blocking collectives  99 us (18%)
  local copies, waits for them, and re-layouts  47.2 us (8%)
  matrix products  27.1 us (5%)
  starting transfers between devices  20.1 us (4%)
  between operations  14.2 us (3%)
    reduce_scatter x1, waiting for transfers between devices, on_device(): lax.psum_scatter(lax.dot_general(grad_part, gated_rows, (((1,), (1,)), ((...  158 us
    all_gather x1, waiting for transfers between devices, on_device(): lax.all_gather(w_out, 'ctx', axis=0, tiled=True)  105 us
    all_to_all x1, blocking collectives, on_device(): lax.all_to_all(conv_grad, 'ctx', split_axis=0, concat_axis=1, tiled=True)  54.2 us
    all_to_all x1, blocking collectives, on_device(): lax.all_to_all(jnp.stack(jnp.split(mixed.astype(jnp.bfloat16), lax.axis_s...  44.9 us
    all_to_all x1, waiting for transfers between devices, on_device(): lax.all_to_all(kv_product, 'ctx', split_axis=0, concat_axis=1, tiled=True)  31.2 us
    all_gather x1, waiting for transfers between devices, on_device(): grad_full = lax.all_gather(out_grad, 'fsdp', axis=0, tiled=True)  30.9 us
    all_to_all x1, waiting for transfers between devices, on_device(): lax.all_to_all(signal_grad.astype(jnp.bfloat16), 'ctx', split_axis=1, con...  15 us
    reshape x4, local copies, waits for them, and re-layouts, make_band(): window_cut.reshape(channels, tap_count, 2 * tap_count - 1)[:, :, :tap_count]  14.5 us
  transfers between devices with their start and end apart: 5, of which 5 were waited for; matrix products, arithmetic and copies ran while one was open for 13% of the time, Pallas kernels for 0%

profile of v1, /device:TPU:32, one launch (start us, length us, event | category | flops | bytes accessed | tf_op | source)
XLA Modules:
  0.0 552.3 jit_solution(14414515279667108531)
XLA Ops:
  7.9 13.1 %all-to-all-start = ((bf16[32,16,1024]{2,1,0:T(8,128)(2,1)}), bf16[32,16,1024]{2,1,0:T(8,128)(2,1)S(1)}, u32[]{:S(2)}, u32[]{:S(2)}) async-start(bf16[32,16,1024]{2,1,0:T(8,128)(2,1)} %bitcast.207), calls=%async_computation | async-start | bytes 2097152 | tf_op jit(solution)/shard_map/all_to_all | solution.py:60
  22.2 3.4 reshape.70
  26.9 4.6 reshape.68
  31.5 31.2 %all-to-all-done = bf16[32,16,1024]{2,1,0:T(8,128)(2,1)S(1)} async-done(((bf16[32,16,1024]{2,1,0:T(8,128)(2,1)}), bf16[32,16,1024]{2,1,0:T(8,128)(2,1)S(1)}, u32[]{:S(2)}, u32[]{:S(2)}) %all-to-all-start) | async-done | bytes 1048608 | tf_op jit(solution)/shard_map/all_to_all | solution.py:60
  67.8 1.6 copy.31
  70.5 44.9 %all_to_all.53 = bf16[32,16,1024]{2,1,0:T(8,128)(2,1)S(1)} all-to-all(bf16[32,16,1024]{2,1,0:T(8,128)(2,1)S(1)} %constant_dynamic-update-slice_fusion), channel_id=1, replica_groups=mesh['ctx'=32,'fsdp'=8] {'ctx'}, dimensions={0} | all-to-all | bytes 2097152 | tf_op jit(solution)/shard_map/all_to_all | solution.py:70
  115.4 30.9 %all-gather.5.cloned.1.call-done = bf16[4096,1024]{1,0:T(8,128)(2,1)} async-done(((bf16[512,1024]{1,0:T(8,128)(2,1)}), bf16[4096,1024]{1,0:T(8,128)(2,1)}) %all-gather.5.cloned.1.call-update) | async-done | bytes 8388624 | tf_op jit(solution)/shard_map/all_gather | solution.py:50
  146.3 11.5 %convolution_bitcast_fusion = f32[4096,512]{0,1:T(8,128)} fusion(bf16[4096,1024]{1,0:T(8,128)(2,1)} %all-gather.5.cloned.1.call-done, bf16[512,1024]{1,0:T(8,128)(2,1)S(1)} %bitcast.208, bf16[512,1024]{1,0:T(8,128)(2,1)} %param.6), kind=kOutput, calls=%fused_computation | convolution fusion | flops 4297064448 | bytes 18874368 | tf_op jit(solution)/shard_map/dot_general | solution.py:89
  157.8 104.9 %all-gather.3.cloned.1.call-done = bf16[4096,512]{1,0:T(8,128)(2,1)} async-done(((bf16[128,512]{1,0:T(8,128)(2,1)}), bf16[4096,512]{1,0:T(8,128)(2,1)}) %all-gather.3.cloned.1.call-update) | async-done | bytes 4194320 | tf_op jit(solution)/shard_map/all_gather | solution.py:53
  262.6 10.7 %fusion = (bf16[512,1024]{1,0:T(8,128)(2,1)S(1)}, f32[512,1024]{1,0:T(8,128)}) fusion(bf16[512,1024]{1,0:T(8,128)(2,1)} %param.6, bf16[32,16,1024]{2,1,0:T(8,128)(2,1)S(1)} %all_to_all.53, bf16[4096,512]{1,0:T(8,128)(2,1)} %all-gather.3.cloned.1.call-done, bf16[4096,1024]{1,0:T(8,128)(2,1)} %all-gather.5.cloned.1.call-done), kind=kOutput, calls=%fused_computation.4 | convolution fusion | flops 4297588736 | bytes 17825792 | tf_op jit(solution)/shard_map/dot_general | solution.py:52
  273.3 54.2 %all_to_all.54 = bf16[32,16,1024]{2,1,0:T(8,128)(2,1)S(1)} all-to-all(bf16[32,16,1024]{2,1,0:T(8,128)(2,1)S(1)} %bitcast.209), channel_id=1, replica_groups=mesh['ctx'=32,'fsdp'=8] {'ctx'}, dimensions={0} | all-to-all | bytes 2097152 | tf_op jit(solution)/shard_map/all_to_all | solution.py:61
  335.2 1.5 copy.34
  336.7 6.9 %all-to-all-start.3 = ((bf16[16,32,1024]{2,0,1:T(8,128)(2,1)}), bf16[16,32,1024]{2,0,1:T(8,128)(2,1)}, u32[]{:S(2)}, u32[]{:S(2)}) async-start(bf16[16,32,1024]{2,0,1:T(8,128)(2,1)} %copy.34), calls=%async_computation.3 | async-start | bytes 2097152 | tf_op jit(solution)/shard_map/all_to_all | solution.py:78
  345.5 2.8 pad.18.clone
  348.3 4.1 reshape.74
  352.4 3.1 pad.19
  355.4 2.8 reshape.75
  358.2 1.8 reduce_sum.19
  360.8 2.5 reshape.72
  363.3 3.1 pad.17
  366.4 1.7 reshape.73
  368.9 15.0 %all-to-all-done.3 = bf16[16,32,1024]{2,0,1:T(8,128)(2,1)} async-done(((bf16[16,32,1024]{2,0,1:T(8,128)(2,1)}), bf16[16,32,1024]{2,0,1:T(8,128)(2,1)}, u32[]{:S(2)}, u32[]{:S(2)}) %all-to-all-start.3) | async-done | bytes 1048608 | tf_op jit(solution)/shard_map/all_to_all | solution.py:78
  383.9 157.8 %reduce-scatter.2.cloned.1.call-done = f32[128,512]{0,1:T(8,128)} async-done(((f32[4096,512]{0,1:T(8,128)}), f32[128,512]{0,1:T(8,128)}) %reduce-scatter.2.cloned.1.call-update) | async-done | bytes 262160 | tf_op jit(solution)/shard_map/reduce_scatter | solution.py:88
  543.5 2.3 copy.82
  (70 shorter events, 21.9 us)
Async XLA Ops:
  7.2 14.6 %copy-start.2 = (bf16[1,1,16,128]{3,2,1,0:T(8,128)(2,1)S(1)}, bf16[1,1,16,128]{3,2,1,0:T(8,128)(2,1)}, u32[]{:S(2)}) copy-start(bf16[1,1,16,128]{3,2,1,0:T(8,128)(2,1)} %param.9) | copy-start | bytes 12292
  7.2 139.1 %all-gather.5.cloned.1.call-start = ((), (), s32[]{:S(2)}) async-start(), calls=%async_computation.6 | async-start | bytes 9437184 | tf_op jit(solution)/shard_map/all_gather | solution.py:50
  7.9 54.8 %all-to-all-start = ((bf16[32,16,1024]{2,1,0:T(8,128)(2,1)}), bf16[32,16,1024]{2,1,0:T(8,128)(2,1)S(1)}, u32[]{:S(2)}, u32[]{:S(2)}) async-start(bf16[32,16,1024]{2,1,0:T(8,128)(2,1)} %bitcast.207), calls=%async_computation | async-start | bytes 2097152 | tf_op jit(solution)/shard_map/all_to_all | solution.py:60
  21.0 241.7 %all-gather.3.cloned.1.call-start = ((), (), s32[]{:S(2)}) async-start(), calls=%async_computation.5 | async-start | bytes 4325376 | tf_op jit(solution)/shard_map/all_gather | solution.py:53
  21.7 520.0 %reduce-scatter.2.cloned.1.call-start = ((), (), s32[]{:S(2)}) async-start(), calls=%async_computation.7 | async-start | bytes 8650752 | tf_op jit(solution)/shard_map/reduce_scatter | solution.py:88
  31.5 34.8 %copy-start = (bf16[16,128,255]{2,1,0:T(8,128)(2,1)}, bf16[16,128,255]{2,1,0:T(8,128)(2,1)S(1)}, u32[]{:S(2)}) copy-start(bf16[16,128,255]{2,1,0:T(8,128)(2,1)S(1)} %reshape.68) | copy-start | bytes 3133444
  330.6 1.2 copy-start.1
  336.7 47.1 %all-to-all-start.3 = ((bf16[16,32,1024]{2,0,1:T(8,128)(2,1)}), bf16[16,32,1024]{2,0,1:T(8,128)(2,1)}, u32[]{:S(2)}, u32[]{:S(2)}) async-start(bf16[16,32,1024]{2,0,1:T(8,128)(2,1)} %copy.34), calls=%async_computation.3 | async-start | bytes 2097152 | tf_op jit(solution)/shard_map/all_to_all | solution.py:78
Sparse Core Ops, SparseCore 0:
  9.8 136.4 all-gather.4
  149.8 112.8 all-gather.2
  265.2 276.4 reduce-scatter.1
